TPU v7x, 256 devices: a whole 4x4x8 slice. The times are simulated.
256 devices in a mesh: band: 4 (over y_lo, core), slab: 64 (over z, y_hi, x).
Axes of the slice: x: 4, y: 4 (y_hi: 2, y_lo: 2; y = y_hi * 2 + y_lo), z: 8, core: 2. Of those that a mesh axis runs over, the one named last changes fastest.
Arguments:
- bands: float32 [8, 192, 192, 192], P('band', 'slab'), may hold values from -8 to 8
- occupied: float32 [16, 192, 192, 192], P('band', 'slab'), may hold values from -8 to 8
- occ_index: int32 [2], replicated, may hold values from 0 to 15
- band_pick: int32 [8], P('band'), may hold values from 0 to 1
Outputs:
- exchange_out: float32 [8, 192, 192, 192], P('band', 'slab')
All inputs are finite; a program needn't handle non-finite values.
Results may differ from a plain program's by a relative error of at most 0.0001.
Values sent between devices are 32-bit elements; how exact they have to be, the bound alone decides.
A program may use at most 64 MiB of HBM per device.

v0:
```python
import math
import jax
import jax.numpy as jnp
from jax import lax
from jax.sharding import PartitionSpec as P

grid_step = 0.25
omega = 0.106


def broadcast(x, axis, root):
    mine = lax.axis_index(axis) == root
    return lax.psum(jnp.where(mine, x, jnp.zeros_like(x)), axis)


def wave_squared(length):
    modes = jnp.arange(length, dtype=jnp.int32)
    signed = jnp.where(modes <= length // 2, modes, modes - length)
    wave = 2.0 * math.pi / (length * grid_step) * signed.astype(jnp.float32)
    return wave * wave


def screened(squares):
    nonzero = jnp.where(squares > 0, squares, jnp.ones_like(squares))
    value = 4.0 * math.pi * (1.0 - jnp.exp(-squares / (4.0 * omega * omega))) / nonzero
    return jnp.where(squares > 0, value, jnp.full_like(squares, math.pi / (omega * omega)))


def cas_matrix(length):
    indices = jnp.arange(length, dtype=jnp.int32)
    product = indices[:, None] * indices[None, :] % length
    phases = 2.0 * math.pi / length * product.astype(jnp.float32)
    return jnp.cos(phases) + jnp.sin(phases)


def along_z(values, matrix):
    return jnp.einsum("pxyz,zk->pxyk", values, matrix, precision=lax.Precision.HIGHEST)


def along_y(values, matrix):
    return jnp.einsum("pxyz,yk->pxkz", values, matrix, precision=lax.Precision.HIGHEST)


def along_x(values, matrix):
    return jnp.einsum("pxyz,xk->pkyz", values, matrix, precision=lax.Precision.HIGHEST)


def shards(bands, occupied, occ_index, band_pick):
    points = bands.shape[2]
    planes = bands.shape[1]
    window = occ_index.shape[0]
    per_group = occupied.shape[0]
    matrix = cas_matrix(points)
    squares = wave_squared(points)
    offset = lax.axis_index("slab") * planes
    row_squares = lax.dynamic_slice_in_dim(squares, offset, planes)
    kernel = screened(squares[:, None, None] + row_squares[None, :, None] + squares[None, None, :])
    kernel = kernel / float(points * points * points)
    targets = jnp.take(bands, band_pick, axis=0)

    def fetch_orbital(turn):
        which = occ_index[turn]
        owner_group = which // per_group
        own_orbital = lax.dynamic_index_in_dim(occupied, which % per_group, 0, keepdims=False)
        return broadcast(own_orbital, "band", owner_group)

    def to_spectrum(density):
        return along_y(along_z(density, matrix), matrix)

    def from_spectrum(spectrum):
        return along_z(along_y(spectrum, matrix), matrix)

    def convolve(pencil):
        return along_x(kernel[None] * along_x(pencil, matrix), matrix)

    def back_each(pencil):
        return lax.all_to_all(convolve(pencil), "slab", split_axis=1, concat_axis=2, tiled=True)

    def update(turn, total):
        orbital = fetch_orbital(turn)
        density = targets * orbital[None]
        filtered = back_each(
            lax.all_to_all(to_spectrum(density), "slab", split_axis=2, concat_axis=1, tiled=True)
        )
        return total - from_spectrum(filtered) * orbital[None]

    result = lax.fori_loop(0, window, update, jnp.zeros(targets.shape, jnp.float32))
    return result


def solution(mesh):
    placed = (P("band", "slab", None, None), P("band", "slab", None, None), P(), P("band"))
    return jax.shard_map(
        shards, mesh=mesh, in_specs=placed, out_specs=P("band", "slab", None, None), check_vma=False
    )
```

profile of v0, /device:TPU:6, one launch (start us, length us, event | category | flops | bytes accessed | tf_op | source)
XLA Modules:
  0.0 321.0 jit_solution(7959825404634566891)
XLA Ops:
  6.5 0.1 dynamic_slice.24
  6.6 0.1 broadcast_add_fusion
  6.7 0.7 compare_select_fusion.1
  7.4 0.4 copy-done
  7.8 0.6 gather_fusion
  8.5 0.0 copy-done.6
  8.5 0.2 broadcast_select_fusion
  8.7 0.5 copy-done.7
  9.1 305.0 %while.17 = (s32[]{:T(128)}, f32[2,3,192,192]{3,2,1,0:T(8,128)}, s32[2]{0:T(128)S(1)}, f32[4,3,192,192]{3,2,1,0:T(8,128)}, f32[2,3,192,192]{3,2,1,0:T(8,128)S(1)...) while((s32[]{:T(128)}, f32[2,3,192,192]{3,2,1,0:T(8,128)}, ...), condition=%wide.region_2.3_spmd.clone.clone, body=%wide.region_0.2_spmd.clone.clone.sunk | while | flops 3062292480 | bytes 46599840 | solution.py:87
  9.1 0.6 dynamic_slice.33
  12.0 1.9 select_bitcast_fusion.2
  13.9 0.0 all-reduce.2.cloned.1.call-update
  14.0 46.4 %all-reduce.2.cloned.1.call-done = f32[3,192,192]{2,1,0:T(8,128)} async-done(((f32[3,192,192]{2,1,0:T(8,128)}), f32[3,192,192]{2,1,0:T(8,128)}) %all-reduce.2.cloned.1.call-update) | async-done | bytes 442384 | tf_op jit(solution)/shard_map/while/body/eval_jaxpr/psum | solution.py:13
  60.4 3.1 fusion.81
  63.5 1.9 convolution_bitcast_fusion.7
  65.4 1.6 copy.44
  67.0 12.7 %all-to-all-start = ((f32[2,3,192,192]{3,0,1,2:T(2,128)}), f32[2,3,192,192]{3,0,1,2:T(2,128)S(1)}, u32[]{:S(2)}, u32[]{:S(2)}) async-start(f32[2,3,192,192]{3,0,1,2:T(2,128)} %copy.44), calls=%async_computation | async-start | bytes 2359296 | tf_op jit(solution)/shard_map/while/body/eval_jaxpr/all_to_all | solution.py:83
  79.7 0.3 fusion.82
  80.0 32.1 %all-to-all-done = f32[2,3,192,192]{3,0,1,2:T(2,128)S(1)} async-done(((f32[2,3,192,192]{3,0,1,2:T(2,128)}), f32[2,3,192,192]{3,0,1,2:T(2,128)S(1)}, u32[]{:S(2)}, u32[]{:S(2)}) %all-to-all-start) | async-done | bytes 884768 | tf_op jit(solution)/shard_map/while/body/eval_jaxpr/all_to_all | solution.py:83
  112.1 0.4 copy.45
  112.5 3.0 fusion.83
  115.5 1.9 convolution_bitcast_fusion.8
  117.4 1.6 copy.46
  119.0 7.2 %all-to-all-start.1 = ((f32[2,192,3,192]{3,0,2,1:T(2,128)}), f32[2,192,3,192]{3,0,2,1:T(2,128)S(1)}, u32[]{:S(2)}, u32[]{:S(2)}) async-start(f32[2,192,3,192]{3,0,2,1:T(2,128)} %copy.46), calls=%async_computation.1 | async-start | bytes 2359296 | tf_op jit(solution)/shard_map/while/body/eval_jaxpr/all_to_all | solution.py:77
  126.3 31.1 %all-to-all-done.1 = f32[2,192,3,192]{3,0,2,1:T(2,128)S(1)} async-done(((f32[2,192,3,192]{3,0,2,1:T(2,128)}), f32[2,192,3,192]{3,0,2,1:T(2,128)S(1)}, u32[]{:S(2)}, u32[]{:S(2)}) %all-to-all-start.1) | async-done | bytes 884768 | tf_op jit(solution)/shard_map/while/body/eval_jaxpr/all_to_all | solution.py:77
  157.3 0.4 copy.47
  157.8 3.0 convolution_bitcast_fusion.9
  160.8 3.4 %fusion.84 = f32[2,3,192,192]{3,2,1,0:T(8,128)S(1)} fusion(f32[2,3,192,192]{2,3,1,0:T(8,128)S(1)} %convolution_bitcast_fusion.9, f32[2,3,192,192]{3,2,1,0:T(8,128)S(1)} %copy-done.4, f32[3,192,192]{2,1,0:T(8,128)S(1)} %copy-done.1, pred[]{:T(512)S(6)} %compare.14), kind=kOutput, calls=%fused_computation.4.clone.1 | convolution fusion | flops 510640128 | bytes 3096577 | tf_op jit(solution)/shard_map/while/body/eval_jaxpr/pxyz,zk->pxyk/dot_general | solution.py:37
  164.2 1.0 copy-done.5
  165.2 0.6 dynamic_slice.33
  168.1 1.9 select_bitcast_fusion.2
  170.1 39.2 %all-reduce.2.cloned.1.call-done = f32[3,192,192]{2,1,0:T(8,128)} async-done(((f32[3,192,192]{2,1,0:T(8,128)}), f32[3,192,192]{2,1,0:T(8,128)}) %all-reduce.2.cloned.1.call-update) | async-done | bytes 442384 | tf_op jit(solution)/shard_map/while/body/eval_jaxpr/psum | solution.py:13
  209.2 3.1 fusion.81
  212.4 1.9 convolution_bitcast_fusion.7
  214.3 1.6 copy.44
  215.9 12.7 %all-to-all-start = ((f32[2,3,192,192]{3,0,1,2:T(2,128)}), f32[2,3,192,192]{3,0,1,2:T(2,128)S(1)}, u32[]{:S(2)}, u32[]{:S(2)}) async-start(f32[2,3,192,192]{3,0,1,2:T(2,128)} %copy.44), calls=%async_computation | async-start | bytes 2359296 | tf_op jit(solution)/shard_map/while/body/eval_jaxpr/all_to_all | solution.py:83
  228.5 0.3 fusion.82
  228.9 32.1 %all-to-all-done = f32[2,3,192,192]{3,0,1,2:T(2,128)S(1)} async-done(((f32[2,3,192,192]{3,0,1,2:T(2,128)}), f32[2,3,192,192]{3,0,1,2:T(2,128)S(1)}, u32[]{:S(2)}, u32[]{:S(2)}) %all-to-all-start) | async-done | bytes 884768 | tf_op jit(solution)/shard_map/while/body/eval_jaxpr/all_to_all | solution.py:83
  260.9 0.4 copy.45
  261.3 3.0 fusion.83
  264.4 1.9 convolution_bitcast_fusion.8
  266.3 1.6 copy.46
  267.9 7.2 %all-to-all-start.1 = ((f32[2,192,3,192]{3,0,2,1:T(2,128)}), f32[2,192,3,192]{3,0,2,1:T(2,128)S(1)}, u32[]{:S(2)}, u32[]{:S(2)}) async-start(f32[2,192,3,192]{3,0,2,1:T(2,128)} %copy.46), calls=%async_computation.1 | async-start | bytes 2359296 | tf_op jit(solution)/shard_map/while/body/eval_jaxpr/all_to_all | solution.py:77
  275.1 31.1 %all-to-all-done.1 = f32[2,192,3,192]{3,0,2,1:T(2,128)S(1)} async-done(((f32[2,192,3,192]{3,0,2,1:T(2,128)}), f32[2,192,3,192]{3,0,2,1:T(2,128)S(1)}, u32[]{:S(2)}, u32[]{:S(2)}) %all-to-all-start.1) | async-done | bytes 884768 | tf_op jit(solution)/shard_map/while/body/eval_jaxpr/all_to_all | solution.py:77
  306.2 0.4 copy.47
  306.6 3.0 convolution_bitcast_fusion.9
  309.7 3.4 %fusion.84 = f32[2,3,192,192]{3,2,1,0:T(8,128)S(1)} fusion(f32[2,3,192,192]{2,3,1,0:T(8,128)S(1)} %convolution_bitcast_fusion.9, f32[2,3,192,192]{3,2,1,0:T(8,128)S(1)} %copy-done.4, f32[3,192,192]{2,1,0:T(8,128)S(1)} %copy-done.1, pred[]{:T(512)S(6)} %compare.14), kind=kOutput, calls=%fused_computation.4.clone.1 | convolution fusion | flops 510640128 | bytes 3096577 | tf_op jit(solution)/shard_map/while/body/eval_jaxpr/pxyz,zk->pxyk/dot_general | solution.py:37
  313.1 1.0 copy-done.5
  (28 shorter events, 0.1 us)
Async XLA Ops:
  6.5 1.3 copy-start
  7.8 0.7 copy-start.6
  8.5 0.7 copy-start.7
  9.1 51.2 %copy-start.2 = (f32[2,3,192,192]{3,2,1,0:T(8,128)}, f32[2,3,192,192]{3,2,1,0:T(8,128)S(1)}, u32[]{:S(2)}) copy-start(f32[2,3,192,192]{3,2,1,0:T(8,128)S(1)} %get-tuple-element.343) | copy-start | bytes 2654212 | tf_op jit(solution)/shard_map/while
  9.1 51.2 %all-reduce.2.cloned.1.call-start = ((), (), s32[]{:S(2)}) async-start(), calls=%async_computation.2 | async-start | bytes 1179648 | tf_op jit(solution)/shard_map/while/body/eval_jaxpr/psum | solution.py:13
  67.0 45.1 %all-to-all-start = ((f32[2,3,192,192]{3,0,1,2:T(2,128)}), f32[2,3,192,192]{3,0,1,2:T(2,128)S(1)}, u32[]{:S(2)}, u32[]{:S(2)}) async-start(f32[2,3,192,192]{3,0,1,2:T(2,128)} %copy.44), calls=%async_computation | async-start | bytes 2359296 | tf_op jit(solution)/shard_map/while/body/eval_jaxpr/all_to_all | solution.py:83
  119.0 38.3 %all-to-all-start.1 = ((f32[2,192,3,192]{3,0,2,1:T(2,128)}), f32[2,192,3,192]{3,0,2,1:T(2,128)S(1)}, u32[]{:S(2)}, u32[]{:S(2)}) async-start(f32[2,192,3,192]{3,0,2,1:T(2,128)} %copy.46), calls=%async_computation.1 | async-start | bytes 2359296 | tf_op jit(solution)/shard_map/while/body/eval_jaxpr/all_to_all | solution.py:77
  157.7 3.1 copy-start.1
  157.8 3.1 copy-start.4
  160.8 4.4 %copy-start.3 = (f32[2,3,192,192]{3,2,1,0:T(8,128)S(1)}, f32[2,3,192,192]{3,2,1,0:T(8,128)}, u32[]{:S(2)}) copy-start(f32[2,3,192,192]{3,2,1,0:T(8,128)} %copy-done.2) | copy-start | bytes 2654212 | tf_op jit(solution)/shard_map/while
  164.2 1.0 copy-start.5
  165.2 44.0 %copy-start.2 = (f32[2,3,192,192]{3,2,1,0:T(8,128)}, f32[2,3,192,192]{3,2,1,0:T(8,128)S(1)}, u32[]{:S(2)}) copy-start(f32[2,3,192,192]{3,2,1,0:T(8,128)S(1)} %get-tuple-element.343) | copy-start | bytes 2654212 | tf_op jit(solution)/shard_map/while
  165.2 44.0 %all-reduce.2.cloned.1.call-start = ((), (), s32[]{:S(2)}) async-start(), calls=%async_computation.2 | async-start | bytes 1179648 | tf_op jit(solution)/shard_map/while/body/eval_jaxpr/psum | solution.py:13
  215.9 45.1 %all-to-all-start = ((f32[2,3,192,192]{3,0,1,2:T(2,128)}), f32[2,3,192,192]{3,0,1,2:T(2,128)S(1)}, u32[]{:S(2)}, u32[]{:S(2)}) async-start(f32[2,3,192,192]{3,0,1,2:T(2,128)} %copy.44), calls=%async_computation | async-start | bytes 2359296 | tf_op jit(solution)/shard_map/while/body/eval_jaxpr/all_to_all | solution.py:83
  267.9 38.3 %all-to-all-start.1 = ((f32[2,192,3,192]{3,0,2,1:T(2,128)}), f32[2,192,3,192]{3,0,2,1:T(2,128)S(1)}, u32[]{:S(2)}, u32[]{:S(2)}) async-start(f32[2,192,3,192]{3,0,2,1:T(2,128)} %copy.46), calls=%async_computation.1 | async-start | bytes 2359296 | tf_op jit(solution)/shard_map/while/body/eval_jaxpr/all_to_all | solution.py:77
  306.6 3.1 copy-start.1
  306.6 3.1 copy-start.4
  309.7 4.4 %copy-start.3 = (f32[2,3,192,192]{3,2,1,0:T(8,128)S(1)}, f32[2,3,192,192]{3,2,1,0:T(8,128)}, u32[]{:S(2)}) copy-start(f32[2,3,192,192]{3,2,1,0:T(8,128)} %copy-done.2) | copy-start | bytes 2654212 | tf_op jit(solution)/shard_map/while
  313.1 1.0 copy-start.5
Sparse Core Ops, SparseCore 0:
  14.1 46.2 all-reduce.1
  170.2 38.9 all-reduce.1
where the time goes:
time: 322 us; the launch traced here: 321 us
  waiting for transfers between devices  212 us (66%)
  starting transfers between devices  39.9 us (12%)
  matrix products  32.8 us (10%)
  between operations  13.4 us (4%)
  local copies, waits for them, and re-layouts  12.8 us (4%)
  other arithmetic  5.52 us (2%)
  loops' own time  4.72 us (1%)
    psum x2, waiting for transfers between devices, broadcast(): return lax.psum(jnp.where(mine, x, jnp.zeros_like(x)), axis)  85.5 us
    all_to_all x2, waiting for transfers between devices, update(): lax.all_to_all(to_spectrum(density), 'slab', split_axis=2, concat_axis=1,...  64.2 us
    all_to_all x2, waiting for transfers between devices, back_each(): lax.all_to_all(convolve(pencil), 'slab', split_axis=1, concat_axis=2, til...  62.1 us
    all_to_all x2, starting transfers between devices, update(): lax.all_to_all(to_spectrum(density), 'slab', split_axis=2, concat_axis=1,...  25.4 us
    all_to_all x2, starting transfers between devices, back_each(): lax.all_to_all(convolve(pencil), 'slab', split_axis=1, concat_axis=2, til...  14.5 us
    dot_general x4, matrix products, along_z(): jnp.einsum('pxyz,zk->pxyk', values, matrix, precision=lax.Precision.HIGHEST)  13 us
    dot_general x4, matrix products, along_x(): jnp.einsum('pxyz,xk->pkyz', values, matrix, precision=lax.Precision.HIGHEST)  9.88 us
    dot_general x4, matrix products, along_y(): jnp.einsum('pxyz,yk->pxkz', values, matrix, precision=lax.Precision.HIGHEST)  9.88 us
  transfers between devices with their start and end apart: 6, of which 6 were waited for; matrix products, arithmetic and copies ran while one was open for 0% of the time, Pallas kernels for 0%

commit v1 on v0

--- a/solution.py
+++ b/solution.py
@@ -10,7 +10,7 @@
 
 def broadcast(x, axis, root):
     mine = lax.axis_index(axis) == root
-    return lax.psum(jnp.where(mine, x, jnp.zeros_like(x)), axis)
+    return jnp.sum(lax.all_gather(jnp.where(mine, x, jnp.zeros_like(x)), axis), axis=0)
 
 
 def wave_squared(length):

time: 322 us -> 306 us (0.950)
  waiting for transfers between devices: 212 us -> 192 us
  other arithmetic: 5.52 us -> 9.28 us
    psum x2 -> x0, waiting for transfers between devices: 85.5 us -> none  [broadcast(): return lax.psum(jnp.where(mine, x, jnp.zeros_like(x)), axis)]
    all_gather x0 -> x2, waiting for transfers between devices: none -> 65.7 us  [broadcast(): lax.all_gather(jnp.where(mine, x, jnp.zeros_like(x)), axis)]
    reduce_sum x0 -> x2, other arithmetic: none -> 3.81 us  [broadcast(): jnp.sum(lax.all_gather(jnp.where(mine, x, jnp.zeros_like(x)), axis), axis=0)]
where the time goes in v1:
time: 306 us; the launch traced here: 305 us
  waiting for transfers between devices  192 us (63%)
  starting transfers between devices  40.6 us (13%)
  matrix products  30.7 us (10%)
  between operations  13.4 us (4%)
  local copies, waits for them, and re-layouts  13.1 us (4%)
  other arithmetic  9.28 us (3%)
  loops' own time  5.85 us (2%)
    all_gather x2, waiting for transfers between devices, broadcast(): lax.all_gather(jnp.where(mine, x, jnp.zeros_like(x)), axis)  65.7 us
    all_to_all x2, waiting for transfers between devices, update(): lax.all_to_all(to_spectrum(density), 'slab', split_axis=2, concat_axis=1,...  63.9 us
    all_to_all x2, waiting for transfers between devices, back_each(): lax.all_to_all(convolve(pencil), 'slab', split_axis=1, concat_axis=2, til...  62.5 us
    all_to_all x2, starting transfers between devices, update(): lax.all_to_all(to_spectrum(density), 'slab', split_axis=2, concat_axis=1,...  25.4 us
    all_to_all x2, starting transfers between devices, back_each(): lax.all_to_all(convolve(pencil), 'slab', split_axis=1, concat_axis=2, til...  15.3 us
    dot_general x4, matrix products, along_z(): jnp.einsum('pxyz,zk->pxyk', values, matrix, precision=lax.Precision.HIGHEST)  10.9 us
    dot_general x4, matrix products, along_y(): jnp.einsum('pxyz,yk->pxkz', values, matrix, precision=lax.Precision.HIGHEST)  9.88 us
    dot_general x4, matrix products, along_x(): jnp.einsum('pxyz,xk->pkyz', values, matrix, precision=lax.Precision.HIGHEST)  9.88 us
  transfers between devices with their start and end apart: 6, of which 6 were waited for; matrix products, arithmetic and copies ran while one was open for 0% of the time, Pallas kernels for 0%

profile of v1, /device:TPU:6, one launch (start us, length us, event | category | flops | bytes accessed | tf_op | source)
XLA Modules:
  0.0 305.0 jit_solution(1228042453816683156)
XLA Ops:
  6.5 0.1 dynamic_slice.24
  6.6 0.1 broadcast_add_fusion
  6.7 0.7 compare_select_fusion.1
  7.4 0.4 copy-done
  7.8 0.6 gather_fusion
  8.5 0.2 broadcast_select_fusion
  8.7 0.5 copy-done.6
  9.1 289.1 %while.17 = (s32[]{:T(128)}, f32[2,3,192,192]{3,2,1,0:T(8,128)}, s32[2]{0:T(128)S(1)}, f32[4,3,192,192]{3,2,1,0:T(8,128)}, f32[2,3,192,192]{3,2,1,0:T(8,128)S(1)...) while((s32[]{:T(128)}, f32[2,3,192,192]{3,2,1,0:T(8,128)}, ...), condition=%wide.region_2.3_spmd.clone.clone, body=%wide.region_0.2_spmd.clone.clone.sunk | while | flops 3062513664 | bytes 51465872 | solution.py:87
  9.1 0.8 dynamic_slice.33
  12.7 1.9 dynamic-slice_select_fusion.2
  14.6 36.5 %all-gather.2.cloned.1.call-done = f32[4,3,192,192]{3,2,1,0:T(8,128)} async-done(((f32[1,3,192,192]{3,2,1,0:T(8,128)}), f32[4,3,192,192]{3,2,1,0:T(8,128)}) %all-gather.2.cloned.1.call-update) | async-done | bytes 1769488 | tf_op jit(solution)/shard_map/while/body/eval_jaxpr/all_gather | solution.py:13
  51.1 1.9 reduce_sum.19
  53.0 2.1 fusion.81
  55.1 1.9 convolution_bitcast_fusion.7
  57.0 1.6 copy.44
  58.6 12.7 %all-to-all-start = ((f32[2,3,192,192]{3,0,1,2:T(2,128)}), f32[2,3,192,192]{3,0,1,2:T(2,128)S(1)}, u32[]{:S(2)}, u32[]{:S(2)}) async-start(f32[2,3,192,192]{3,0,1,2:T(2,128)} %copy.44), calls=%async_computation | async-start | bytes 2359296 | tf_op jit(solution)/shard_map/while/body/eval_jaxpr/all_to_all | solution.py:83
  71.3 0.3 fusion.82
  71.6 32.0 %all-to-all-done = f32[2,3,192,192]{3,0,1,2:T(2,128)S(1)} async-done(((f32[2,3,192,192]{3,0,1,2:T(2,128)}), f32[2,3,192,192]{3,0,1,2:T(2,128)S(1)}, u32[]{:S(2)}, u32[]{:S(2)}) %all-to-all-start) | async-done | bytes 884768 | tf_op jit(solution)/shard_map/while/body/eval_jaxpr/all_to_all | solution.py:83
  103.6 0.4 copy.45
  104.0 3.0 fusion.83
  107.0 1.9 convolution_bitcast_fusion.8
  108.9 1.6 copy.46
  110.5 7.6 %all-to-all-start.1 = ((f32[2,192,3,192]{3,0,2,1:T(2,128)}), f32[2,192,3,192]{3,0,2,1:T(2,128)S(1)}, u32[]{:S(2)}, u32[]{:S(2)}) async-start(f32[2,192,3,192]{3,0,2,1:T(2,128)} %copy.46), calls=%async_computation.1 | async-start | bytes 2359296 | tf_op jit(solution)/shard_map/while/body/eval_jaxpr/all_to_all | solution.py:77
  118.2 31.2 %all-to-all-done.1 = f32[2,192,3,192]{3,0,2,1:T(2,128)S(1)} async-done(((f32[2,192,3,192]{3,0,2,1:T(2,128)}), f32[2,192,3,192]{3,0,2,1:T(2,128)S(1)}, u32[]{:S(2)}, u32[]{:S(2)}) %all-to-all-start.1) | async-done | bytes 884768 | tf_op jit(solution)/shard_map/while/body/eval_jaxpr/all_to_all | solution.py:77
  149.4 0.4 copy.47
  149.8 3.0 convolution_bitcast_fusion.9
  152.9 3.4 %fusion.84 = f32[2,3,192,192]{3,2,1,0:T(8,128)S(1)} fusion(f32[2,3,192,192]{2,3,1,0:T(8,128)S(1)} %convolution_bitcast_fusion.9, f32[2,3,192,192]{3,2,1,0:T(8,128)S(1)} %copy-done.3, f32[3,192,192]{2,1,0:T(8,128)S(1)} %reduce_sum.19, pred[]{:T(512)S(6)} %compare.14), kind=kOutput, calls=%fused_computation.4.clone.1 | convolution fusion | flops 510640128 | bytes 3096577 | tf_op jit(solution)/shard_map/while/body/eval_jaxpr/pxyz,zk->pxyk/dot_general | solution.py:37
  156.3 1.0 copy-done.4
  157.3 0.8 dynamic_slice.33
  160.9 1.9 dynamic-slice_select_fusion.2
  162.8 29.2 %all-gather.2.cloned.1.call-done = f32[4,3,192,192]{3,2,1,0:T(8,128)} async-done(((f32[1,3,192,192]{3,2,1,0:T(8,128)}), f32[4,3,192,192]{3,2,1,0:T(8,128)}) %all-gather.2.cloned.1.call-update) | async-done | bytes 1769488 | tf_op jit(solution)/shard_map/while/body/eval_jaxpr/all_gather | solution.py:13
  192.0 1.9 reduce_sum.19
  193.9 2.1 fusion.81
  196.0 1.9 convolution_bitcast_fusion.7
  197.9 1.6 copy.44
  199.5 12.7 %all-to-all-start = ((f32[2,3,192,192]{3,0,1,2:T(2,128)}), f32[2,3,192,192]{3,0,1,2:T(2,128)S(1)}, u32[]{:S(2)}, u32[]{:S(2)}) async-start(f32[2,3,192,192]{3,0,1,2:T(2,128)} %copy.44), calls=%async_computation | async-start | bytes 2359296 | tf_op jit(solution)/shard_map/while/body/eval_jaxpr/all_to_all | solution.py:83
  212.2 0.3 fusion.82
  212.5 32.0 %all-to-all-done = f32[2,3,192,192]{3,0,1,2:T(2,128)S(1)} async-done(((f32[2,3,192,192]{3,0,1,2:T(2,128)}), f32[2,3,192,192]{3,0,1,2:T(2,128)S(1)}, u32[]{:S(2)}, u32[]{:S(2)}) %all-to-all-start) | async-done | bytes 884768 | tf_op jit(solution)/shard_map/while/body/eval_jaxpr/all_to_all | solution.py:83
  244.5 0.4 copy.45
  244.9 3.0 fusion.83
  247.9 1.9 convolution_bitcast_fusion.8
  249.8 1.6 copy.46
  251.4 7.6 %all-to-all-start.1 = ((f32[2,192,3,192]{3,0,2,1:T(2,128)}), f32[2,192,3,192]{3,0,2,1:T(2,128)S(1)}, u32[]{:S(2)}, u32[]{:S(2)}) async-start(f32[2,192,3,192]{3,0,2,1:T(2,128)} %copy.46), calls=%async_computation.1 | async-start | bytes 2359296 | tf_op jit(solution)/shard_map/while/body/eval_jaxpr/all_to_all | solution.py:77
  259.1 31.2 %all-to-all-done.1 = f32[2,192,3,192]{3,0,2,1:T(2,128)S(1)} async-done(((f32[2,192,3,192]{3,0,2,1:T(2,128)}), f32[2,192,3,192]{3,0,2,1:T(2,128)S(1)}, u32[]{:S(2)}, u32[]{:S(2)}) %all-to-all-start.1) | async-done | bytes 884768 | tf_op jit(solution)/shard_map/while/body/eval_jaxpr/all_to_all | solution.py:77
  290.3 0.4 copy.47
  290.7 3.0 convolution_bitcast_fusion.9
  293.8 3.4 %fusion.84 = f32[2,3,192,192]{3,2,1,0:T(8,128)S(1)} fusion(f32[2,3,192,192]{2,3,1,0:T(8,128)S(1)} %convolution_bitcast_fusion.9, f32[2,3,192,192]{3,2,1,0:T(8,128)S(1)} %copy-done.3, f32[3,192,192]{2,1,0:T(8,128)S(1)} %reduce_sum.19, pred[]{:T(512)S(6)} %compare.14), kind=kOutput, calls=%fused_computation.4.clone.1 | convolution fusion | flops 510640128 | bytes 3096577 | tf_op jit(solution)/shard_map/while/body/eval_jaxpr/pxyz,zk->pxyk/dot_general | solution.py:37
  297.2 1.0 copy-done.4
  (26 shorter events, 0.1 us)
Async XLA Ops:
  6.5 1.3 copy-start
  7.8 0.7 copy-start.5
  8.5 0.7 copy-start.6
  9.1 43.9 %copy-start.1 = (f32[2,3,192,192]{3,2,1,0:T(8,128)}, f32[2,3,192,192]{3,2,1,0:T(8,128)S(1)}, u32[]{:S(2)}) copy-start(f32[2,3,192,192]{3,2,1,0:T(8,128)S(1)} %get-tuple-element.345) | copy-start | bytes 2654212 | tf_op jit(solution)/shard_map/while
  9.1 42.0 %all-gather.2.cloned.1.call-start = ((), (), s32[]{:S(2)}) async-start(), calls=%async_computation.2 | async-start | bytes 2949120 | tf_op jit(solution)/shard_map/while/body/eval_jaxpr/all_gather | solution.py:13
  58.6 44.9 %all-to-all-start = ((f32[2,3,192,192]{3,0,1,2:T(2,128)}), f32[2,3,192,192]{3,0,1,2:T(2,128)S(1)}, u32[]{:S(2)}, u32[]{:S(2)}) async-start(f32[2,3,192,192]{3,0,1,2:T(2,128)} %copy.44), calls=%async_computation | async-start | bytes 2359296 | tf_op jit(solution)/shard_map/while/body/eval_jaxpr/all_to_all | solution.py:83
  110.5 38.9 %all-to-all-start.1 = ((f32[2,192,3,192]{3,0,2,1:T(2,128)}), f32[2,192,3,192]{3,0,2,1:T(2,128)S(1)}, u32[]{:S(2)}, u32[]{:S(2)}) async-start(f32[2,192,3,192]{3,0,2,1:T(2,128)} %copy.46), calls=%async_computation.1 | async-start | bytes 2359296 | tf_op jit(solution)/shard_map/while/body/eval_jaxpr/all_to_all | solution.py:77
  149.8 3.1 %copy-start.3 = (f32[2,3,192,192]{3,2,1,0:T(8,128)S(1)}, f32[2,3,192,192]{3,2,1,0:T(8,128)}, u32[]{:S(2)}) copy-start(f32[2,3,192,192]{3,2,1,0:T(8,128)} %get-tuple-element.326) | copy-start | bytes 2654212 | tf_op jit(solution)/shard_map/while
  152.9 4.4 %copy-start.2 = (f32[2,3,192,192]{3,2,1,0:T(8,128)S(1)}, f32[2,3,192,192]{3,2,1,0:T(8,128)}, u32[]{:S(2)}) copy-start(f32[2,3,192,192]{3,2,1,0:T(8,128)} %copy-done.1) | copy-start | bytes 2654212 | tf_op jit(solution)/shard_map/while
  156.3 1.0 copy-start.4
  157.3 36.6 %copy-start.1 = (f32[2,3,192,192]{3,2,1,0:T(8,128)}, f32[2,3,192,192]{3,2,1,0:T(8,128)S(1)}, u32[]{:S(2)}) copy-start(f32[2,3,192,192]{3,2,1,0:T(8,128)S(1)} %get-tuple-element.345) | copy-start | bytes 2654212 | tf_op jit(solution)/shard_map/while
  157.3 34.7 %all-gather.2.cloned.1.call-start = ((), (), s32[]{:S(2)}) async-start(), calls=%async_computation.2 | async-start | bytes 2949120 | tf_op jit(solution)/shard_map/while/body/eval_jaxpr/all_gather | solution.py:13
  199.5 45.0 %all-to-all-start = ((f32[2,3,192,192]{3,0,1,2:T(2,128)}), f32[2,3,192,192]{3,0,1,2:T(2,128)S(1)}, u32[]{:S(2)}, u32[]{:S(2)}) async-start(f32[2,3,192,192]{3,0,1,2:T(2,128)} %copy.44), calls=%async_computation | async-start | bytes 2359296 | tf_op jit(solution)/shard_map/while/body/eval_jaxpr/all_to_all | solution.py:83
  251.4 38.9 %all-to-all-start.1 = ((f32[2,192,3,192]{3,0,2,1:T(2,128)}), f32[2,192,3,192]{3,0,2,1:T(2,128)S(1)}, u32[]{:S(2)}, u32[]{:S(2)}) async-start(f32[2,192,3,192]{3,0,2,1:T(2,128)} %copy.46), calls=%async_computation.1 | async-start | bytes 2359296 | tf_op jit(solution)/shard_map/while/body/eval_jaxpr/all_to_all | solution.py:77
  290.7 3.1 %copy-start.3 = (f32[2,3,192,192]{3,2,1,0:T(8,128)S(1)}, f32[2,3,192,192]{3,2,1,0:T(8,128)}, u32[]{:S(2)}) copy-start(f32[2,3,192,192]{3,2,1,0:T(8,128)} %get-tuple-element.326) | copy-start | bytes 2654212 | tf_op jit(solution)/shard_map/while
  293.8 4.4 %copy-start.2 = (f32[2,3,192,192]{3,2,1,0:T(8,128)S(1)}, f32[2,3,192,192]{3,2,1,0:T(8,128)}, u32[]{:S(2)}) copy-start(f32[2,3,192,192]{3,2,1,0:T(8,128)} %copy-done.1) | copy-start | bytes 2654212 | tf_op jit(solution)/shard_map/while
  297.2 1.0 copy-start.4
Sparse Core Ops, SparseCore 0:
  14.8 36.3 all-gather.1
  162.9 29.0 all-gather.1
